TPU v7x, 32 devices: a whole 2x2x4 slice. The times are simulated.
32 devices in a mesh: lat: 8 (over y, x, core), lev: 4 (over z).
Axes of the slice: x: 2, y: 2, z: 4, core: 2. Of those that a mesh axis runs over, the one named last changes fastest.
Arguments:
- grid_adjoint: float32 [2, 96, 640, 1280], P(None, 'lev', 'lat'), may hold values from -6 to 6
- trajectory: bfloat16 [2, 96, 640, 1280], P(None, 'lev', 'lat'), may hold values from -5 to 5
- pair_order: int32 [320], replicated, may hold values from 0 to 319, each once
- legendre: bfloat16 [320, 640, 641], P('lat'), may hold values from -0.25 to 0.25
- modes: bfloat16 [96, 96], replicated, may hold values from -0.625 to 0.625
- rates: float32 [96], replicated, may hold values from 0.5 to 50
Outputs:
- grid_out: float32 [2, 96, 640, 1280], P(None, 'lev', 'lat')
Inputs may be any that keep to these rules, and one draw needn't show every extreme that they name: `pair_order`: A permutation: entry s names the pair k and 639 - k whose basis values are row s of legendre.
All inputs are finite; a program needn't handle non-finite values.
Results may differ from a plain program's by a relative error of at most 0.0068.
Values may be sent and summed in bfloat16 or wider, within the bound.
A program may use at most 192 MiB of HBM per device.

v0:
```python
import math
import jax
import jax.numpy as jnp
from jax import lax
from jax.sharding import PartitionSpec as P


def tables(length, number):
    row = lax.broadcasted_iota(jnp.int32, (length, 2 * number), 0)
    col = lax.broadcasted_iota(jnp.int32, (length, 2 * number), 1)
    wavenum = col % number
    phases = 2.0 * math.pi / length * (row * wavenum % length).astype(jnp.float32)
    forward = (jnp.where(col < number, jnp.cos(phases), -jnp.sin(phases)) / length).astype(
        jnp.bfloat16
    )
    inrow = lax.broadcasted_iota(jnp.int32, (2 * number, length), 0)
    position = lax.broadcasted_iota(jnp.int32, (2 * number, length), 1)
    inwave = inrow % number
    inphase = 2.0 * math.pi / length * (position * inwave % length).astype(jnp.float32)
    weights = jnp.where(inwave == 0, 1.0, 2.0).astype(jnp.float32)
    inverse = jnp.where(
        inrow < number, weights * jnp.cos(inphase), -weights * jnp.sin(inphase)
    ).astype(jnp.bfloat16)
    return (forward, inverse)


def degrees(waves_a, truncation):
    column = lax.broadcasted_iota(jnp.int32, (waves_a.shape[0], truncation + 1), 1)
    lower_part = column < (truncation - waves_a)[:, None]
    degree = jnp.where(lower_part, waves_a[:, None] + column, column - 1)
    degree_ratio = (degree * (degree + 1)).astype(jnp.float32) / float(
        truncation * (truncation + 1)
    )
    return (lower_part, degree_ratio)


def per_device(grid_adjoint, trajectory, pair_order, legendre, modes, rates):
    fields, levels, lat_rows, longitudes = grid_adjoint.shape
    wave_count = longitudes // 2
    slot_count = legendre.shape[0]
    lat_count = legendre.shape[1]
    primary = trajectory[0].astype(jnp.float32)
    coupling = trajectory[1].astype(jnp.float32)
    coupled = jnp.stack(
        [
            primary * grid_adjoint[0] + coupling * grid_adjoint[1],
            coupling * grid_adjoint[0] + primary * grid_adjoint[1],
        ]
    ).astype(jnp.bfloat16)
    forward, inverse = tables(longitudes, wave_count)
    fourier_local = jnp.dot(
        coupled.reshape(-1, longitudes), forward, preferred_element_type=jnp.float32
    )
    fourier_local = fourier_local.astype(jnp.bfloat16).reshape(
        fields, levels, lat_rows, 2, wave_count
    )
    column_order = jnp.stack([pair_order, wave_count - 1 - pair_order], axis=1).reshape(-1)
    permuted = jnp.take(fourier_local, column_order, axis=4)
    received_bands = lax.all_to_all(permuted, "lat", split_axis=4, concat_axis=2, tiled=True)
    grouped = received_bands.reshape(fields, levels, lat_count, 2, slot_count, 2)
    band_index = lax.axis_index("lat")
    local_waves = lax.dynamic_slice_in_dim(pair_order, band_index * slot_count, slot_count)
    lower_part, degree_ratio = degrees(local_waves, wave_count)
    products = jnp.einsum(
        "slj,fvlcsh->sfvchj", legendre, grouped, preferred_element_type=jnp.float32
    )
    lower_mask = lower_part[:, None, None, None, :]
    spectral = jnp.where(lower_mask, products[:, :, :, :, 0], products[:, :, :, :, 1])
    damped = spectral[:, 0] / (1.0 + 4.0 * degree_ratio * degree_ratio)[:, None, None, :]
    rounded = spectral[:, 1].astype(jnp.bfloat16)
    level_index = lax.axis_index("lev")
    lev_count = lax.axis_size("lev")
    flattened = jnp.transpose(rounded, (1, 0, 2, 3)).reshape(levels, -1)
    column_total = flattened.shape[1]
    column_width = -(-column_total // lev_count)
    padding = column_width * lev_count - column_total
    padded = jnp.pad(flattened, ((0, 0), (0, padding)))
    columns = lax.all_to_all(padded, "lev", split_axis=1, concat_axis=0, tiled=True)
    ratio_flat = jnp.broadcast_to(
        degree_ratio[:, None, :], (slot_count, 2, wave_count + 1)
    ).reshape(-1)
    ratio_flat = jnp.pad(ratio_flat, (0, padding))
    ratio_piece = lax.dynamic_slice_in_dim(ratio_flat, level_index * column_width, column_width)
    projected = jnp.einsum("km,kn->mn", modes, columns, preferred_element_type=jnp.float32)
    factor = 1.0 / (1.0 + rates[:, None] * ratio_piece[None, :])
    weighted = (projected * factor).astype(jnp.bfloat16)
    solved_columns = jnp.dot(modes, weighted, preferred_element_type=jnp.float32)
    returned_levels = lax.all_to_all(
        solved_columns.astype(jnp.bfloat16), "lev", split_axis=0, concat_axis=1, tiled=True
    ).astype(solved_columns.dtype)
    solved = returned_levels[:, :column_total].reshape(levels, slot_count, 2, wave_count + 1)
    solved = jnp.transpose(solved, (1, 0, 2, 3))
    updated = jnp.stack([damped, solved], axis=1).astype(jnp.bfloat16)
    zero_value = jnp.zeros((), jnp.bfloat16)
    halves = jnp.stack(
        [jnp.where(lower_mask, updated, zero_value), jnp.where(lower_mask, zero_value, updated)],
        axis=-2,
    )
    synthesised = jnp.einsum(
        "slj,sfvchj->fvlcsh", legendre, halves, preferred_element_type=jnp.float32
    )
    synthesised = synthesised.astype(jnp.bfloat16).reshape(
        fields, levels, lat_count, 2, slot_count * 2
    )
    returned = lax.all_to_all(synthesised, "lat", split_axis=2, concat_axis=4, tiled=True)
    inverse_order = (
        jnp.zeros((wave_count,), jnp.int32)
        .at[column_order]
        .set(jnp.arange(wave_count, dtype=jnp.int32))
    )
    natural = jnp.take(returned, inverse_order, axis=4)
    grid_out = jnp.dot(
        natural.reshape(-1, 2 * wave_count), inverse, preferred_element_type=jnp.float32
    )
    return grid_out.reshape(fields, levels, lat_rows, longitudes)


def solution(mesh):
    placed = (
        P(None, "lev", "lat", None),
        P(None, "lev", "lat", None),
        P(),
        P("lat", None, None),
        P(),
        P(),
    )
    return jax.shard_map(
        per_device,
        mesh=mesh,
        in_specs=placed,
        out_specs=P(None, "lev", "lat", None),
        check_vma=False,
    )
```

profile of v0, /device:TPU:0, one launch (start us, length us, event | category | flops | bytes accessed | tf_op | source)
XLA Modules:
  0.0 961.1 jit_solution(389869084658848675)
XLA Ops:
  1.8 14.9 %fusion.9 = (bf16[1,24,80,1280]{3,2,1,0:T(8,128)(2,1)}, bf16[1,24,80,1280]{3,2,1,0:T(8,128)(2,1)}) fusion(f32[2,24,80,1280]{3,2,1,0:T(8,128)} %param.8, bf16[2,24,80,1280]{3,2,1,0:T(8,128)(2,1)} %param.9), kind=kLoop, calls=%fused_computation.25 | loop fusion | flops 24576000 | bytes 39321600 | tf_op jit(solution)/shard_map/convert.8
  16.6 8.6 pad_maximum_fusion.1
  25.3 27.6 %multiply_convert_fusion.4 = bf16[1280,1280]{1,0:T(8,128)(2,1)S(1)} fusion(s32[1280]{0:T(1024)S(1)} %get-tuple-element.14, s32[1280]{0:T(1024)S(1)} %get-tuple-element.15, pred[1280]{0:T(1024)(128)(4,1)S(1)} %get-tuple-element.17, pred[1280]{0:T(1024)(128)(4,1)S(1)} %get-tuple-element.16), kind=kLoop, calls=%fused_computation.47.clone.clone.1 | loop fusion | flops 22937600 | bytes 3289600 | tf_op jit(solution)/shard_map/dot_general | solution.py:51
  52.9 19.0 %convolution_convert_fusion.1 = bf16[3840,1280]{1,0:T(8,128)(2,1)} fusion(bf16[3840,1280]{1,0:T(8,128)(2,1)} %bitcast.82, bf16[1280,1280]{1,0:T(8,128)(2,1)S(1)} %multiply_convert_fusion.4), kind=kOutput, calls=%fused_computation.14 | convolution fusion | flops 12587827200 | bytes 22937600 | tf_op jit(solution)/shard_map/dot_general | solution.py:51
  71.9 19.3 %reshape.233 = bf16[2,24,80,2,640]{4,3,2,1,0:T(2,128)(2,1)} reshape(bf16[3840,1280]{1,0:T(8,128)(2,1)} %convolution_convert_fusion.1) | data formatting | bytes 19660800 | tf_op jit(solution)/shard_map/reshape | solution.py:54
  91.2 25.9 %copy.64 = bf16[2,24,80,2,640]{2,1,3,0,4:T(8,128)(2,1)} copy(bf16[2,24,80,2,640]{4,3,2,1,0:T(2,128)(2,1)} %reshape.233) | data formatting | bytes 19660800 | tf_op jit(solution)/shard_map/reshape | solution.py:54
  117.1 25.2 %gather_fusion = bf16[640,2,24,80,2]{3,2,4,1,0:T(8,128)(2,1)} fusion(bf16[2,24,80,2,640]{2,1,3,0,4:T(8,128)(2,1)} %copy.64, s32[1024]{0:T(1024)S(1)} %pad_clamp_fusion.1), kind=kCustom, calls=%fused_computation.clone | custom fusion | bytes 19663360 | tf_op jit(solution)/shard_map/jit(_take)/gather | solution.py:58
  142.3 14.0 %select_bitcast_fusion.1 = bf16[2,24,80,2,640]{2,1,3,0,4:T(8,128)(2,1)} fusion(bf16[640,2,24,80,2]{3,2,4,1,0:T(8,128)(2,1)} %gather_fusion, pred[640]{0:T(1024)(128)(4,1)S(1)} %compare_and_fusion.1), kind=kLoop, calls=%fused_computation.9 | loop fusion | flops 4915200 | bytes 19661440 | tf_op jit(solution)/shard_map/jit(_take)/select_n | solution.py:58
  156.3 5.6 all-to-all-start
  162.8 172.5 %all-to-all-done = bf16[2,24,80,2,640]{2,1,3,0,4:T(8,128)(2,1)} async-done(((bf16[2,24,80,2,640]{2,1,3,0,4:T(8,128)(2,1)}), bf16[2,24,80,2,640]{2,1,3,0,4:T(8,128)(2,1)}, u32[]{:S(2)}, u32[]{:S(2)}) %all-to-all-start) | async-done | bytes 9830432 | tf_op jit(solution)/shard_map/all_to_all | solution.py:59
  335.4 27.2 %copy.104 = bf16[2,24,80,2,8,80]{2,4,1,5,3,0:T(8,128)(2,1)} copy(bf16[2,24,80,2,8,80]{2,1,3,0,5,4:T(8,128)(2,1)} %bitcast.2) | data formatting | bytes 19660800 | tf_op jit(solution)/shard_map/all_to_all | solution.py:59
  362.6 23.1 %reshape.235 = bf16[2,24,640,2,40,2]{2,1,5,4,3,0:T(8,128)(2,1)} reshape(bf16[2,24,8,80,2,80]{3,2,1,5,4,0:T(8,128)(2,1)} %bitcast.76) | data formatting | bytes 19660800 | tf_op jit(solution)/shard_map/reshape | solution.py:60
  385.6 29.7 %fusion.2 = f32[40,2,24,2,2,641]{5,2,4,3,1,0:T(8,128)} fusion(bf16[40,640,641,1,1,1]{1,0,2,5,4,3:T(8,128)(2,1)} %bitcast.79, bf16[2,24,640,2,40,2]{2,1,5,4,3,0:T(8,128)(2,1)} %reshape.235), kind=kOutput, calls=%fused_computation.5 | convolution fusion | flops 6301286400 | bytes 62341120 | tf_op jit(solution)/shard_map/slj,fvlcsh->sfvchj/dot_general | solution.py:64
  415.3 9.1 fusion.6
  424.5 4.5 copy-done.2
  438.8 15.4 %all-to-all-start.1 = ((bf16[24,4,12820]{2,0,1:T(8,128)(2,1)}), bf16[24,4,12820]{2,0,1:T(8,128)(2,1)S(1)}, u32[]{:S(2)}, u32[]{:S(2)}) async-start(bf16[24,4,12820]{2,0,1:T(8,128)(2,1)} %copy.70), calls=%async_computation.1 | async-start | bytes 4964352 | tf_op jit(solution)/shard_map/all_to_all | solution.py:78
  454.8 52.9 %all-to-all-done.1 = bf16[24,4,12820]{2,0,1:T(8,128)(2,1)S(1)} async-done(((bf16[24,4,12820]{2,0,1:T(8,128)(2,1)}), bf16[24,4,12820]{2,0,1:T(8,128)(2,1)S(1)}, u32[]{:S(2)}, u32[]{:S(2)}) %all-to-all-start.1) | async-done | bytes 2461472 | tf_op jit(solution)/shard_map/all_to_all | solution.py:78
  510.7 4.5 all-to-all-start.2
  518.7 52.7 %all-to-all-done.2 = bf16[4,24,12820]{2,1,0:T(8,128)(2,1)} async-done(((bf16[4,24,12820]{2,1,0:T(8,128)(2,1)}), bf16[4,24,12820]{2,1,0:T(8,128)(2,1)}, u32[]{:S(2)}, u32[]{:S(2)}) %all-to-all-start.2) | async-done | bytes 2461472 | tf_op jit(solution)/shard_map/all_to_all | solution.py:88
  575.5 10.8 %convert_element_type.92 = bf16[24,40,2,641]{3,2,1,0:T(2,128)(2,1)} reshape(bf16[24,4,12820]{2,1,0:T(4,128)(2,1)} %copy.71) | data formatting | bytes 4922880 | tf_op jit(solution)/shard_map/convert_element_type | solution.py:90
  591.3 22.3 %convert_bitcast_fusion = bf16[2,24,640,2,40,2]{2,1,5,3,0,4:T(8,128)(2,1)} fusion(bf16[40,640,641,1,1,1]{1,0,2,5,4,3:T(8,128)(2,1)} %bitcast.80, bf16[40,2,24,2,1,641]{5,2,3,0,4,1:T(8,128)(2,1)S(1)} %get-tuple-element.11, bf16[40,2,24,2,1,641]{5,2,3,0,4,1:T(8,128)(2,1)S(1)} %get-tuple-element.10), kind=kOutput, calls=%fused_computation.31 | convolution fusion | flops 6311124480 | bytes 52495360 | tf_op jit(solution)/shard_map/slj,sfvchj->fvlcsh/dot_general | solution.py:99
  613.6 8.4 copy.75
  622.0 20.1 %copy.76 = bf16[2,24,640,2,80]{4,1,3,0,2:T(8,128)(2,1)} copy(bf16[2,24,640,2,80]{2,1,4,3,0:T(8,128)(2,1)} %bitcast.78) | data formatting | bytes 19660800 | tf_op jit(solution)/shard_map/reshape | solution.py:102
  642.2 6.0 all-to-all-start.3
  652.5 30.0 %fusion.83 = bf16[1280,1280,1,1]{1,0,3,2:T(8,128)(2,1)S(1)} fusion(s32[1280]{0:T(1024)S(1)} %copy-done.6, s32[1280]{0:T(1024)S(1)} %copy-done.8, pred[1280]{0:T(1024)(128)(4,1)S(1)} %copy-done.12, pred[1280]{0:T(1024)(128)(4,1)S(1)} %copy-done.10), kind=kLoop, calls=%fused_computation.59.clone.clone.1 | loop fusion | flops 27852800 | bytes 3289600 | tf_op jit(solution)/shard_map/dot_general | solution.py:112
  682.5 138.4 %all-to-all-done.3 = bf16[2,24,640,2,80]{4,1,3,0,2:T(8,128)(2,1)} async-done(((bf16[2,24,640,2,80]{4,1,3,0,2:T(8,128)(2,1)}), bf16[2,24,640,2,80]{4,1,3,0,2:T(8,128)(2,1)}, u32[]{:S(2)}, u32[]{:S(2)}) %all-to-all-start.3) | async-done | bytes 9830432 | tf_op jit(solution)/shard_map/all_to_all | solution.py:105
  820.9 33.7 %copy.87 = bf16[2,24,80,2,8,80]{2,1,3,0,5,4:T(8,128)(2,1)} copy(bf16[2,24,80,2,8,80]{5,1,3,0,2,4:T(8,128)(2,1)} %bitcast.31) | data formatting | bytes 19660800 | tf_op jit(solution)/shard_map/all_to_all | solution.py:105
  854.6 25.0 %gather_fusion.1 = bf16[640,2,24,80,2]{3,2,4,1,0:T(8,128)(2,1)} fusion(bf16[2,24,80,2,640]{2,1,3,0,4:T(8,128)(2,1)} %bitcast.77, s32[1024]{0:T(1024)S(1)} %pad_clamp_fusion), kind=kCustom, calls=%fused_computation.1.clone | custom fusion | bytes 19663360 | tf_op jit(solution)/shard_map/jit(_take)/gather | solution.py:111
  879.5 14.0 %select_bitcast_fusion = bf16[2,24,80,2,640]{2,1,3,0,4:T(8,128)(2,1)} fusion(bf16[640,2,24,80,2]{3,2,4,1,0:T(8,128)(2,1)} %gather_fusion.1, pred[640]{0:T(1024)(128)(4,1)S(1)} %compare_and_fusion), kind=kLoop, calls=%fused_computation.8 | loop fusion | flops 4915200 | bytes 19661440 | tf_op jit(solution)/shard_map/jit(_take)/select_n | solution.py:111
  893.6 26.9 %copy.79 = bf16[2,24,80,2,640]{4,3,2,1,0:T(2,128)(2,1)} copy(bf16[2,24,80,2,640]{2,1,3,0,4:T(8,128)(2,1)} %select_bitcast_fusion) | data formatting | bytes 19660800 | tf_op jit(solution)/shard_map/jit(_take)/select_n | solution.py:111
  920.5 21.8 %dot_general.28 = bf16[2,24,80,1280]{3,2,1,0:T(8,128)(2,1)} reshape(bf16[2,24,80,2,640]{4,3,2,1,0:T(2,128)(2,1)} %copy.79) | data formatting | bytes 19660800 | tf_op jit(solution)/shard_map/dot_general | solution.py:112
  942.3 18.3 %fusion.33 = f32[2,24,80,1280]{3,2,1,0:T(8,128)} fusion(bf16[2,24,80,1280]{3,2,1,0:T(8,128)(2,1)} %dot_general.28, bf16[1280,1280,1,1]{1,0,3,2:T(8,128)(2,1)S(1)} %fusion.83), kind=kOutput, calls=%fused_computation.60 | convolution fusion | flops 12582912000 | bytes 32768000 | tf_op jit(solution)/shard_map/dot_general | solution.py:112
  (61 shorter events, 32.8 us)
Async XLA Ops:
  0.0 507.7 %copy-start = (bf16[96,96]{1,0:T(8,128)(2,1)S(1)}, bf16[96,96]{1,0:T(8,128)(2,1)}, u32[]{:S(2)}) copy-start(bf16[96,96]{1,0:T(8,128)(2,1)} %param.12) | copy-start | bytes 55300
  0.0 25.3 %copy-start.5 = (s32[1280]{0:T(1024)}, s32[1280]{0:T(1024)S(1)}, u32[]{:S(2)}) copy-start(s32[1280]{0:T(1024)S(1)} %get-tuple-element.14) | copy-start | bytes 15364
  0.0 25.3 %copy-start.7 = (s32[1280]{0:T(1024)}, s32[1280]{0:T(1024)S(1)}, u32[]{:S(2)}) copy-start(s32[1280]{0:T(1024)S(1)} %get-tuple-element.15) | copy-start | bytes 15364
  0.0 25.2 %copy-start.9 = (pred[1280]{0:T(1024)(128)(4,1)}, pred[1280]{0:T(1024)(128)(4,1)S(1)}, u32[]{:S(2)}) copy-start(pred[1280]{0:T(1024)(128)(4,1)S(1)} %get-tuple-element.16) | copy-start | bytes 3844
  0.1 25.2 %copy-start.11 = (pred[1280]{0:T(1024)(128)(4,1)}, pred[1280]{0:T(1024)(128)(4,1)S(1)}, u32[]{:S(2)}) copy-start(pred[1280]{0:T(1024)(128)(4,1)S(1)} %get-tuple-element.17) | copy-start | bytes 3844
  1.6 15.0 %copy-start.3 = (s32[320,2]{1,0:T(8,128)}, s32[320,2]{1,0:T(8,128)S(1)}, u32[]{:S(2)}) copy-start(s32[320,2]{1,0:T(8,128)S(1)} %copy.62) | copy-start | bytes 7684
  156.3 179.0 %all-to-all-start = ((bf16[2,24,80,2,640]{2,1,3,0,4:T(8,128)(2,1)}), bf16[2,24,80,2,640]{2,1,3,0,4:T(8,128)(2,1)}, u32[]{:S(2)}, u32[]{:S(2)}) async-start(bf16[2,24,80,2,640]{2,1,3,0,4:T(8,128)(2,1)} %select_bitcast_fusion.1), calls=%async_computation | async-start | bytes 31457280 | tf_op jit(solution)/shard_map/all_to_all | solution.py:59
  424.5 4.5 copy-start.2
  435.4 72.3 %copy-start.13 = (f32[96]{0:T(128)S(1)}, f32[96]{0:T(128)}, u32[]{:S(2)}) copy-start(f32[96]{0:T(128)} %param.13) | copy-start | bytes 1156
  438.8 68.9 %all-to-all-start.1 = ((bf16[24,4,12820]{2,0,1:T(8,128)(2,1)}), bf16[24,4,12820]{2,0,1:T(8,128)(2,1)S(1)}, u32[]{:S(2)}, u32[]{:S(2)}) async-start(bf16[24,4,12820]{2,0,1:T(8,128)(2,1)} %copy.70), calls=%async_computation.1 | async-start | bytes 4964352 | tf_op jit(solution)/shard_map/all_to_all | solution.py:78
  510.7 60.6 %all-to-all-start.2 = ((bf16[4,24,12820]{2,1,0:T(8,128)(2,1)}), bf16[4,24,12820]{2,1,0:T(8,128)(2,1)}, u32[]{:S(2)}, u32[]{:S(2)}) async-start(bf16[4,24,12820]{2,1,0:T(8,128)(2,1)} %bitcast.84), calls=%async_computation.2 | async-start | bytes 4964352 | tf_op jit(solution)/shard_map/all_to_all | solution.py:88
  642.1 6.0 copy-start.4
  642.1 10.4 %copy-start.6 = (s32[1280]{0:T(1024)S(1)}, s32[1280]{0:T(1024)}, u32[]{:S(2)}) copy-start(s32[1280]{0:T(1024)} %copy-done.5) | copy-start | bytes 15364
  642.1 10.4 %copy-start.8 = (s32[1280]{0:T(1024)S(1)}, s32[1280]{0:T(1024)}, u32[]{:S(2)}) copy-start(s32[1280]{0:T(1024)} %copy-done.7) | copy-start | bytes 15364
  642.1 10.4 %copy-start.10 = (pred[1280]{0:T(1024)(128)(4,1)S(1)}, pred[1280]{0:T(1024)(128)(4,1)}, u32[]{:S(2)}) copy-start(pred[1280]{0:T(1024)(128)(4,1)} %copy-done.9) | copy-start | bytes 3844
  642.1 10.4 %copy-start.12 = (pred[1280]{0:T(1024)(128)(4,1)S(1)}, pred[1280]{0:T(1024)(128)(4,1)}, u32[]{:S(2)}) copy-start(pred[1280]{0:T(1024)(128)(4,1)} %copy-done.11) | copy-start | bytes 3844
  642.2 178.7 %all-to-all-start.3 = ((bf16[2,24,640,2,80]{4,1,3,0,2:T(8,128)(2,1)}), bf16[2,24,640,2,80]{4,1,3,0,2:T(8,128)(2,1)}, u32[]{:S(2)}, u32[]{:S(2)}) async-start(bf16[2,24,640,2,80]{4,1,3,0,2:T(8,128)(2,1)} %copy.76), calls=%async_computation.3 | async-start | bytes 31457280 | tf_op jit(solution)/shard_map/all_to_all | solution.py:105
  942.3 18.3 %copy-start.1 = (bf16[96,96]{1,0:T(8,128)(2,1)S(1)}, bf16[96,96]{1,0:T(8,128)(2,1)}, u32[]{:S(2)}) copy-start(bf16[96,96]{1,0:T(8,128)(2,1)} %param.12) | copy-start | bytes 55300
where the time goes:
time: 973 us; the launch traced here: 961 us
  waiting for transfers between devices  416 us (43%)
  local copies, waits for them, and re-layouts  294 us (30%)
  other arithmetic  125 us (13%)
  matrix products  92.3 us (9%)
  starting transfers between devices  31.6 us (3%)
    all_to_all x1, waiting for transfers between devices, per_device(): lax.all_to_all(permuted, 'lat', split_axis=4, concat_axis=2, tiled=True)  173 us
    all_to_all x1, waiting for transfers between devices, per_device(): lax.all_to_all(synthesised, 'lat', split_axis=2, concat_axis=4, tiled=True)  138 us
    all_to_all x1, waiting for transfers between devices, per_device(): lax.all_to_all(padded, 'lev', split_axis=1, concat_axis=0, tiled=True)  52.9 us
    all_to_all x1, waiting for transfers between devices, per_device(): lax.all_to_all(solved_columns.astype(jnp.bfloat16), 'lev', split_axis=0,...  52.7 us
    reshape x2, local copies, waits for them, and re-layouts, per_device(): fourier_local.astype(jnp.bfloat16)  45.2 us
    all_to_all x1, local copies, waits for them, and re-layouts, per_device(): lax.all_to_all(synthesised, 'lat', split_axis=2, concat_axis=4, tiled=True)  33.7 us
    dot_general x1, other arithmetic, per_device(): jnp.dot(natural.reshape(-1, 2 * wave_count), inverse, preferred_element_t...  30 us
    dot_general x1, matrix products, per_device(): jnp.einsum('slj,fvlcsh->sfvchj', legendre, grouped, preferred_element_typ...  29.7 us
  transfers between devices with their start and end apart: 4, of which 4 were waited for; matrix products, arithmetic and copies ran while one was open for 4% of the time, Pallas kernels for 0%

commit v1 on v0

--- a/solution.py
+++ b/solution.py
@@ -3,6 +3,7 @@
 import jax.numpy as jnp
 from jax import lax
 from jax.sharding import PartitionSpec as P
+from jax.lax import all_to_all, axis_size
 
 
 def tables(length, number):
@@ -56,7 +57,15 @@
     )
     column_order = jnp.stack([pair_order, wave_count - 1 - pair_order], axis=1).reshape(-1)
     permuted = jnp.take(fourier_local, column_order, axis=4)
-    received_bands = lax.all_to_all(permuted, "lat", split_axis=4, concat_axis=2, tiled=True)
+    received_bands = jnp.concatenate(
+        all_to_all(
+            jnp.stack(jnp.split(permuted, axis_size("lat"), axis=4), axis=0),
+            axis_name="lat",
+            split_axis=0,
+            concat_axis=0,
+        ),
+        2,
+    )
     grouped = received_bands.reshape(fields, levels, lat_count, 2, slot_count, 2)
     band_index = lax.axis_index("lat")
     local_waves = lax.dynamic_slice_in_dim(pair_order, band_index * slot_count, slot_count)

time: 973 us -> 977 us (level)
  local copies, waits for them, and re-layouts: 294 us -> 307 us
    all_to_all x1 -> x0, local copies, waits for them, and re-layouts: 27.2 us -> none  [per_device(): lax.all_to_all(permuted, 'lat', split_axis=4, concat_axis=2, tiled=True)]
    another operation x0 -> x2, local copies, waits for them, and re-layouts: none -> 24.7 us  [the longest x1 23.1 us: per_device(): received_bands.reshape(fields, levels, lat_count, 2, slot_count, 2)]
    unnamed x28 -> x33, local copies, waits for them, and re-layouts: 4.56 us -> 15.8 us
where the time goes in v1:
time: 977 us; the launch traced here: 964 us
  waiting for transfers between devices  421 us (43%)
  local copies, waits for them, and re-layouts  307 us (31%)
  other arithmetic  121 us (12%)
  matrix products  92.3 us (9%)
  starting transfers between devices  22.4 us (2%)
    all_to_all x1, waiting for transfers between devices, per_device(): all_to_all(jnp.stack(jnp.split(permuted, axis_size('lat'), axis=4), axis=...  173 us
    all_to_all x1, waiting for transfers between devices, per_device(): lax.all_to_all(synthesised, 'lat', split_axis=2, concat_axis=4, tiled=True)  143 us
    all_to_all x1, waiting for transfers between devices, per_device(): lax.all_to_all(padded, 'lev', split_axis=1, concat_axis=0, tiled=True)  52.9 us
    all_to_all x1, waiting for transfers between devices, per_device(): lax.all_to_all(solved_columns.astype(jnp.bfloat16), 'lev', split_axis=0,...  52.7 us
    reshape x2, local copies, waits for them, and re-layouts, per_device(): fourier_local.astype(jnp.bfloat16)  45.2 us
    all_to_all x1, local copies, waits for them, and re-layouts, per_device(): lax.all_to_all(synthesised, 'lat', split_axis=2, concat_axis=4, tiled=True)  33.7 us
    dot_general x1, other arithmetic, per_device(): jnp.dot(natural.reshape(-1, 2 * wave_count), inverse, preferred_element_t...  30 us
    dot_general x1, matrix products, per_device(): jnp.einsum('slj,fvlcsh->sfvchj', legendre, grouped, preferred_element_typ...  29.7 us
  transfers between devices with their start and end apart: 4, of which 4 were waited for; matrix products, arithmetic and copies ran while one was open for 4% of the time, Pallas kernels for 0%

profile of v1, /device:TPU:0, one launch (start us, length us, event | category | flops | bytes accessed | tf_op | source)
XLA Modules:
  0.0 964.4 jit_solution(2943579033215104258)
XLA Ops:
  1.9 14.9 %fusion.9 = (bf16[1,24,80,1280]{3,2,1,0:T(8,128)(2,1)}, bf16[1,24,80,1280]{3,2,1,0:T(8,128)(2,1)}) fusion(f32[2,24,80,1280]{3,2,1,0:T(8,128)} %param.8, bf16[2,24,80,1280]{3,2,1,0:T(8,128)(2,1)} %param.9), kind=kLoop, calls=%fused_computation.24 | loop fusion | flops 24576000 | bytes 39321600 | tf_op jit(solution)/shard_map/convert.8
  16.8 8.6 pad_maximum_fusion.1
  25.4 27.6 %multiply_convert_fusion.4 = bf16[1280,1280]{1,0:T(8,128)(2,1)S(1)} fusion(s32[1280]{0:T(1024)S(1)} %get-tuple-element.14, s32[1280]{0:T(1024)S(1)} %get-tuple-element.15, pred[1280]{0:T(1024)(128)(4,1)S(1)} %get-tuple-element.17, pred[1280]{0:T(1024)(128)(4,1)S(1)} %get-tuple-element.16), kind=kLoop, calls=%fused_computation.46.clone.clone.1 | loop fusion | flops 22937600 | bytes 3289600 | tf_op jit(solution)/shard_map/dot_general | solution.py:52
  53.0 19.0 %convolution_convert_fusion.1 = bf16[3840,1280]{1,0:T(8,128)(2,1)} fusion(bf16[3840,1280]{1,0:T(8,128)(2,1)} %bitcast.110, bf16[1280,1280]{1,0:T(8,128)(2,1)S(1)} %multiply_convert_fusion.4), kind=kOutput, calls=%fused_computation.13 | convolution fusion | flops 12587827200 | bytes 22937600 | tf_op jit(solution)/shard_map/dot_general | solution.py:52
  72.0 19.3 %reshape.232 = bf16[2,24,80,2,640]{4,3,2,1,0:T(2,128)(2,1)} reshape(bf16[3840,1280]{1,0:T(8,128)(2,1)} %convolution_convert_fusion.1) | data formatting | bytes 19660800 | tf_op jit(solution)/shard_map/reshape | solution.py:55
  91.3 25.9 %copy.64 = bf16[2,24,80,2,640]{2,1,3,0,4:T(8,128)(2,1)} copy(bf16[2,24,80,2,640]{4,3,2,1,0:T(2,128)(2,1)} %reshape.232) | data formatting | bytes 19660800 | tf_op jit(solution)/shard_map/reshape | solution.py:55
  122.2 25.0 %gather_fusion = bf16[640,2,24,80,2]{3,2,4,1,0:T(8,128)(2,1)} fusion(bf16[2,24,80,2,640]{2,1,3,0,4:T(8,128)(2,1)} %copy.64, s32[1024]{0:T(1024)S(1)} %get-tuple-element.19), kind=kCustom, calls=%fused_computation.clone | custom fusion | bytes 19663360 | tf_op jit(solution)/shard_map/jit(_take)/gather | solution.py:59
  147.1 8.8 select_bitcast_fusion.1
  168.8 6.1 all-to-all-start
  175.7 172.5 %all-to-all-done = bf16[8,2,24,80,2,80]{3,2,4,1,5,0:T(8,128)(2,1)} async-done(((bf16[8,2,24,80,2,80]{3,2,4,1,5,0:T(8,128)(2,1)}), bf16[8,2,24,80,2,80]{3,2,4,1,5,0:T(8,128)(2,1)}, u32[]{:S(2)}, u32[]{:S(2)}) %all-to-all-start) | async-done | bytes 9830432 | tf_op jit(solution)/shard_map/all_to_all | solution.py:61
  348.3 27.2 %copy.65 = bf16[2,24,8,80,2,80]{3,2,1,5,4,0:T(8,128)(2,1)} copy(bf16[2,24,8,80,2,80]{3,1,4,0,5,2:T(8,128)(2,1)} %bitcast.10) | data formatting | bytes 19660800 | tf_op jit(solution)/shard_map/reshape | solution.py:60
  375.5 23.1 %reshape_reshape.3 = bf16[2,24,640,2,40,2]{2,1,5,4,3,0:T(8,128)(2,1)} reshape(bf16[2,24,8,80,2,80]{3,2,1,5,4,0:T(8,128)(2,1)} %copy.65) | data formatting | bytes 19660800 | tf_op jit(solution)/shard_map/reshape;reshape | solution.py:69
  398.5 29.7 %fusion.2 = f32[40,2,24,2,2,641]{5,2,4,3,1,0:T(8,128)} fusion(bf16[40,640,641,1,1,1]{1,0,2,5,4,3:T(8,128)(2,1)} %bitcast.107, bf16[2,24,640,2,40,2]{2,1,5,4,3,0:T(8,128)(2,1)} %reshape_reshape.3), kind=kOutput, calls=%fused_computation.5 | convolution fusion | flops 6301286400 | bytes 62341120 | tf_op jit(solution)/shard_map/slj,fvlcsh->sfvchj/dot_general | solution.py:73
  428.2 9.1 fusion.6
  437.4 4.5 copy-done.2
  451.7 5.8 all-to-all-start.1
  458.2 52.9 %all-to-all-done.1 = bf16[24,4,12820]{2,0,1:T(8,128)(2,1)S(1)} async-done(((bf16[24,4,12820]{2,0,1:T(8,128)(2,1)}), bf16[24,4,12820]{2,0,1:T(8,128)(2,1)S(1)}, u32[]{:S(2)}, u32[]{:S(2)}) %all-to-all-start.1) | async-done | bytes 2461472 | tf_op jit(solution)/shard_map/all_to_all | solution.py:87
  514.1 4.5 all-to-all-start.2
  522.0 52.7 %all-to-all-done.2 = bf16[4,24,12820]{2,1,0:T(8,128)(2,1)} async-done(((bf16[4,24,12820]{2,1,0:T(8,128)(2,1)}), bf16[4,24,12820]{2,1,0:T(8,128)(2,1)}, u32[]{:S(2)}, u32[]{:S(2)}) %all-to-all-start.2) | async-done | bytes 2461472 | tf_op jit(solution)/shard_map/all_to_all | solution.py:97
  578.8 10.8 %convert_element_type.92 = bf16[24,40,2,641]{3,2,1,0:T(2,128)(2,1)} reshape(bf16[24,4,12820]{2,1,0:T(4,128)(2,1)} %copy.71) | data formatting | bytes 4922880 | tf_op jit(solution)/shard_map/convert_element_type | solution.py:99
  594.6 22.3 %convert_bitcast_fusion = bf16[2,24,640,2,40,2]{2,1,5,3,0,4:T(8,128)(2,1)} fusion(bf16[40,640,641,1,1,1]{1,0,2,5,4,3:T(8,128)(2,1)} %bitcast.108, bf16[40,2,24,2,1,641]{5,2,3,0,4,1:T(8,128)(2,1)S(1)} %get-tuple-element.11, bf16[40,2,24,2,1,641]{5,2,3,0,4,1:T(8,128)(2,1)S(1)} %get-tuple-element.10), kind=kOutput, calls=%fused_computation.30 | convolution fusion | flops 6311124480 | bytes 52495360 | tf_op jit(solution)/shard_map/slj,sfvchj->fvlcsh/dot_general | solution.py:108
  617.0 8.4 copy.75
  625.4 20.1 %copy.76 = bf16[2,24,640,2,80]{4,1,3,0,2:T(8,128)(2,1)} copy(bf16[2,24,640,2,80]{2,1,4,3,0:T(8,128)(2,1)} %bitcast.106) | data formatting | bytes 19660800 | tf_op jit(solution)/shard_map/reshape | solution.py:111
  645.5 6.0 all-to-all-start.3
  651.5 30.0 %fusion.91 = bf16[1280,1280,1,1]{1,0,3,2:T(8,128)(2,1)S(1)} fusion(s32[1280]{0:T(1024)S(1)} %copy-done.5, s32[1280]{0:T(1024)S(1)} %copy-done.7, pred[1280]{0:T(1024)(128)(4,1)S(1)} %copy-done.11, pred[1280]{0:T(1024)(128)(4,1)S(1)} %copy-done.9), kind=kLoop, calls=%fused_computation.58.clone.clone.1 | loop fusion | flops 27852800 | bytes 3289600 | tf_op jit(solution)/shard_map/dot_general | solution.py:121
  681.5 142.7 %all-to-all-done.3 = bf16[2,24,640,2,80]{4,1,3,0,2:T(8,128)(2,1)} async-done(((bf16[2,24,640,2,80]{4,1,3,0,2:T(8,128)(2,1)}), bf16[2,24,640,2,80]{4,1,3,0,2:T(8,128)(2,1)}, u32[]{:S(2)}, u32[]{:S(2)}) %all-to-all-start.3) | async-done | bytes 9830432 | tf_op jit(solution)/shard_map/all_to_all | solution.py:114
  824.2 33.7 %copy.87 = bf16[2,24,80,2,8,80]{2,1,3,0,5,4:T(8,128)(2,1)} copy(bf16[2,24,80,2,8,80]{5,1,3,0,2,4:T(8,128)(2,1)} %bitcast.38) | data formatting | bytes 19660800 | tf_op jit(solution)/shard_map/all_to_all | solution.py:114
  857.9 25.0 %gather_fusion.1 = bf16[640,2,24,80,2]{3,2,4,1,0:T(8,128)(2,1)} fusion(bf16[2,24,80,2,640]{2,1,3,0,4:T(8,128)(2,1)} %bitcast.105, s32[1024]{0:T(1024)S(1)} %copy-done.3), kind=kCustom, calls=%fused_computation.1.clone | custom fusion | bytes 19663360 | tf_op jit(solution)/shard_map/jit(_take)/gather | solution.py:120
  882.9 14.0 %select_bitcast_fusion = bf16[2,24,80,2,640]{2,1,3,0,4:T(8,128)(2,1)} fusion(bf16[640,2,24,80,2]{3,2,4,1,0:T(8,128)(2,1)} %gather_fusion.1, pred[640]{0:T(1024)(128)(4,1)S(1)} %compare_and_fusion), kind=kLoop, calls=%fused_computation.7 | loop fusion | flops 4915200 | bytes 19661440 | tf_op jit(solution)/shard_map/jit(_take)/select_n | solution.py:120
  896.9 26.9 %copy.79 = bf16[2,24,80,2,640]{4,3,2,1,0:T(2,128)(2,1)} copy(bf16[2,24,80,2,640]{2,1,3,0,4:T(8,128)(2,1)} %select_bitcast_fusion) | data formatting | bytes 19660800 | tf_op jit(solution)/shard_map/jit(_take)/select_n | solution.py:120
  923.8 21.8 %dot_general.28 = bf16[2,24,80,1280]{3,2,1,0:T(8,128)(2,1)} reshape(bf16[2,24,80,2,640]{4,3,2,1,0:T(2,128)(2,1)} %copy.79) | data formatting | bytes 19660800 | tf_op jit(solution)/shard_map/dot_general | solution.py:121
  945.7 18.3 %fusion.33 = f32[2,24,80,1280]{3,2,1,0:T(8,128)} fusion(bf16[2,24,80,1280]{3,2,1,0:T(8,128)(2,1)} %dot_general.28, bf16[1280,1280,1,1]{1,0,3,2:T(8,128)(2,1)S(1)} %fusion.91), kind=kOutput, calls=%fused_computation.59 | convolution fusion | flops 12582912000 | bytes 32768000 | tf_op jit(solution)/shard_map/dot_general | solution.py:121
  (66 shorter events, 46.4 us)
Async XLA Ops:
  0.0 511.1 %copy-start = (bf16[96,96]{1,0:T(8,128)(2,1)S(1)}, bf16[96,96]{1,0:T(8,128)(2,1)}, u32[]{:S(2)}) copy-start(bf16[96,96]{1,0:T(8,128)(2,1)} %param.12) | copy-start | bytes 55300
  0.0 25.4 %copy-start.4 = (s32[1280]{0:T(1024)}, s32[1280]{0:T(1024)S(1)}, u32[]{:S(2)}) copy-start(s32[1280]{0:T(1024)S(1)} %get-tuple-element.14) | copy-start | bytes 15364
  0.0 25.4 %copy-start.6 = (s32[1280]{0:T(1024)}, s32[1280]{0:T(1024)S(1)}, u32[]{:S(2)}) copy-start(s32[1280]{0:T(1024)S(1)} %get-tuple-element.15) | copy-start | bytes 15364
  0.0 25.4 %copy-start.8 = (pred[1280]{0:T(1024)(128)(4,1)}, pred[1280]{0:T(1024)(128)(4,1)S(1)}, u32[]{:S(2)}) copy-start(pred[1280]{0:T(1024)(128)(4,1)S(1)} %get-tuple-element.16) | copy-start | bytes 3844
  0.1 25.4 %copy-start.10 = (pred[1280]{0:T(1024)(128)(4,1)}, pred[1280]{0:T(1024)(128)(4,1)S(1)}, u32[]{:S(2)}) copy-start(pred[1280]{0:T(1024)(128)(4,1)S(1)} %get-tuple-element.17) | copy-start | bytes 3844
  168.8 179.5 %all-to-all-start = ((bf16[8,2,24,80,2,80]{3,2,4,1,5,0:T(8,128)(2,1)}), bf16[8,2,24,80,2,80]{3,2,4,1,5,0:T(8,128)(2,1)}, u32[]{:S(2)}, u32[]{:S(2)}) async-start(bf16[8,2,24,80,2,80]{3,2,4,1,5,0:T(8,128)(2,1)} %fusion.54), calls=%async_computation | async-start | bytes 31457280 | tf_op jit(solution)/shard_map/all_to_all | solution.py:61
  437.4 4.5 copy-start.2
  448.3 62.8 %copy-start.12 = (f32[96]{0:T(128)S(1)}, f32[96]{0:T(128)}, u32[]{:S(2)}) copy-start(f32[96]{0:T(128)} %param.13) | copy-start | bytes 1156
  451.7 59.3 %all-to-all-start.1 = ((bf16[24,4,12820]{2,0,1:T(8,128)(2,1)}), bf16[24,4,12820]{2,0,1:T(8,128)(2,1)S(1)}, u32[]{:S(2)}, u32[]{:S(2)}) async-start(bf16[24,4,12820]{2,0,1:T(8,128)(2,1)} %copy.70), calls=%async_computation.1 | async-start | bytes 4964352 | tf_op jit(solution)/shard_map/all_to_all | solution.py:87
  514.1 60.6 %all-to-all-start.2 = ((bf16[4,24,12820]{2,1,0:T(8,128)(2,1)}), bf16[4,24,12820]{2,1,0:T(8,128)(2,1)}, u32[]{:S(2)}, u32[]{:S(2)}) async-start(bf16[4,24,12820]{2,1,0:T(8,128)(2,1)} %bitcast.112), calls=%async_computation.2 | async-start | bytes 4964352 | tf_op jit(solution)/shard_map/all_to_all | solution.py:97
  645.5 6.0 copy-start.5
  645.5 6.0 copy-start.7
  645.5 6.1 copy-start.9
  645.5 6.1 copy-start.11
  645.5 178.7 %all-to-all-start.3 = ((bf16[2,24,640,2,80]{4,1,3,0,2:T(8,128)(2,1)}), bf16[2,24,640,2,80]{4,1,3,0,2:T(8,128)(2,1)}, u32[]{:S(2)}, u32[]{:S(2)}) async-start(bf16[2,24,640,2,80]{4,1,3,0,2:T(8,128)(2,1)} %copy.76), calls=%async_computation.3 | async-start | bytes 31457280 | tf_op jit(solution)/shard_map/all_to_all | solution.py:114
  824.2 33.7 %copy-start.3 = (s32[1024]{0:T(1024)S(1)}, s32[1024]{0:T(1024)}, u32[]{:S(2)}) copy-start(s32[1024]{0:T(1024)} %get-tuple-element.18) | copy-start | bytes 12292
  945.7 18.3 %copy-start.1 = (bf16[96,96]{1,0:T(8,128)(2,1)S(1)}, bf16[96,96]{1,0:T(8,128)(2,1)}, u32[]{:S(2)}) copy-start(bf16[96,96]{1,0:T(8,128)(2,1)} %param.12) | copy-start | bytes 55300
